TPU v7x, 32 devices: a whole 2x2x4 slice. The times are simulated.
32 devices in a mesh: col: 4 (over z), row: 8 (over y, x, core).
Axes of the slice: x: 2, y: 2, z: 4, core: 2. Of those that a mesh axis runs over, the one named last changes fastest.
Arguments:
- affinity: bfloat16 [3840, 128, 128], P(('col', 'row')), may hold values from 0 to 0.015625
- tile_rows: int32 [3840], P(('col', 'row')), may hold values from 0 to 19
- tile_cols: int32 [3840], P(('col', 'row')), may hold values from 0 to 39
- live_tiles: int32 [32], P(('col', 'row')), may hold values from 1 to 120, as said below
- start: float32 [20480, 256], P(('col', 'row')), may hold values from -1500 to 1500
Outputs:
- vectors: float32 [20480, 256], P(('col', 'row'))
- first_passes: float32 [2, 20480, 256], P(None, ('col', 'row'))
Inputs may be any that keep to these rules, and one draw needn't show every extreme that they name: A device's tiles are its slots 0 to live_tiles - 1; later slots are ignored. Some device holds exactly 120 tiles.
All inputs are finite; a program needn't handle non-finite values.
Results may differ from a plain program's by a relative error of at most 0.0003.
Values sent between devices are 32-bit elements; how exact they have to be, the bound alone decides.
No kernel may reach another device: no remote copies, remote signals or barrier semaphores. Data moves between devices by JAX's collectives and lax.ppermute only.
A program may use at most 128 MiB of HBM per device.

v0:
```python
import jax
import jax.numpy as jnp
from jax import lax
from jax.sharding import PartitionSpec as P

ITERS = 2
highest = lax.Precision.HIGHEST


def local_gram(matrix):
    return jnp.dot(matrix.T, matrix, precision=highest, preferred_element_type=jnp.float32)


def inverse_lower(gram):
    lower = jnp.linalg.cholesky(gram)
    return jax.scipy.linalg.solve_triangular(
        lower, jnp.eye(gram.shape[0], dtype=jnp.float32), lower=True
    )


def apply_factor(matrix, inverse):
    return jnp.dot(matrix, inverse.T, precision=highest, preferred_element_type=jnp.float32)


def body(affinity, tile_rows, tile_cols, live_tiles, start):
    n_row = lax.axis_size("row")
    n_col = lax.axis_size("col")
    slot_count = affinity.shape[0]
    tile_size = affinity.shape[1]
    rows_local = start.shape[0]
    vec_count = start.shape[1]
    own_tiles = rows_local // tile_size
    live = (jnp.arange(slot_count) < live_tiles[0]).astype(jnp.float32)
    row_onehot = (jnp.arange(own_tiles * n_col)[:, None] == tile_rows[None, :]).astype(
        jnp.float32
    ) * live[None, :]
    row_sums = jnp.sum(affinity, axis=2, dtype=jnp.float32)
    degree_terms = jnp.dot(
        row_onehot, row_sums, precision=highest, preferred_element_type=jnp.float32
    )
    degree = 1.0 + lax.psum_scatter(degree_terms, "col", scatter_dimension=0, tiled=True).reshape(
        rows_local
    )
    scaling = (1.0 / jnp.sqrt(degree))[:, None]
    squares = affinity.astype(jnp.float32)
    firsts = []
    pending = start
    for step_number in range(ITERS):
        mapped_scaled = scaling * pending
        gathered = lax.all_gather(mapped_scaled, "row", axis=0, tiled=True)
        gathered = gathered.reshape(n_row * own_tiles, tile_size, vec_count)
        picked = gathered[tile_cols]
        products = jnp.einsum(
            "sij,sjk->sik", squares, picked, precision=highest, preferred_element_type=jnp.float32
        )
        terms = jnp.dot(
            row_onehot,
            products.reshape(slot_count, tile_size * vec_count),
            precision=highest,
            preferred_element_type=jnp.float32,
        )
        summed = lax.psum_scatter(terms, "col", scatter_dimension=0, tiled=True)
        raw_image = scaling * (mapped_scaled + summed.reshape(rows_local, vec_count))
        if step_number == 0:
            inner_gram = lax.psum(local_gram(raw_image), ("col", "row"))
            image_block = raw_image
        else:
            raw_gram, pending_gram = lax.psum(
                (local_gram(raw_image), local_gram(pending)), ("col", "row")
            )
            pending_inverse = inverse_lower(pending_gram)
            image_block = apply_factor(raw_image, pending_inverse)
            inner_gram = jnp.dot(
                jnp.dot(
                    pending_inverse, raw_gram, precision=highest, preferred_element_type=jnp.float32
                ),
                pending_inverse.T,
                precision=highest,
                preferred_element_type=jnp.float32,
            )
        pending = apply_factor(image_block, inverse_lower(inner_gram))
        firsts.append(pending)
    final_gram = lax.psum(local_gram(pending), ("col", "row"))
    basis = apply_factor(pending, inverse_lower(final_gram))
    total_images = rows_local * n_row * n_col
    root = jnp.sqrt(jnp.float32(total_images))
    return (root * basis, root * jnp.stack(firsts, axis=0))


def solution(mesh):
    placed = (
        P(("col", "row"), None, None),
        P(("col", "row")),
        P(("col", "row")),
        P(("col", "row")),
        P(("col", "row"), None),
    )
    return jax.shard_map(
        body,
        mesh=mesh,
        in_specs=placed,
        out_specs=(P(("col", "row"), None), P(None, ("col", "row"), None)),
        check_vma=False,
    )
```

profile of v0, /device:TPU:0, one launch (start us, length us, event | category | flops | bytes accessed | tf_op | source)
XLA Modules:
  0.0 1157.0 jit_solution(773065271221598994)
XLA Ops:
  7.9 3.2 convert_reduce_fusion
  11.9 20.4 %all-reduce.1 = f32[20,128]{1,0:T(8,128)S(1)} all-reduce(f32[20,128]{1,0:T(8,128)S(1)} %fusion.55), channel_id=2, replica_groups=mesh['col'=4,'row'=8] {'col'}, use_global_device_ids=true, to_apply=%region_1.0.clone | all-reduce | flops 2560 | bytes 20480
  32.4 1.4 fusion.81
  34.4 2.1 broadcast_multiply_fusion.1
  36.6 39.3 %all-gather.3.cloned.1.call-done = f32[5120,256]{1,0:T(8,128)} async-done(((f32[640,256]{1,0:T(8,128)}), f32[5120,256]{1,0:T(8,128)}) %all-gather.3.cloned.1.call-update) | async-done | bytes 5242896 | tf_op jit(solution)/shard_map/all_gather | solution.py:50
  75.9 12.1 %gather_fusion = f32[120,128,256]{2,1,0:T(8,128)} fusion(f32[40,128,256]{2,1,0:T(8,128)} %bitcast.166, s32[1024]{0:T(1024)S(1)} %pad_clamp_fusion), kind=kCustom, calls=%fused_computation | custom fusion | bytes 31457760 | tf_op jit(solution)/shard_map/gather | solution.py:52
  88.0 20.2 %convolution_bitcast_fusion.1 = f32[120,128,256]{1,2,0:T(8,128)} fusion(f32[120,128,256]{2,1,0:T(8,128)} %gather_fusion, bf16[120,128,128]{2,1,0:T(8,128)(2,1)} %param.8), kind=kOutput, calls=%fused_computation.11 | convolution fusion | flops 6039797760 | bytes 35389440 | tf_op jit(solution)/shard_map/sij,sjk->sik/dot_general | solution.py:53
  108.2 15.7 %copy.41 = f32[15,8,128,256]{3,1,2,0:T(8,128)} copy(f32[15,8,128,256]{2,3,1,0:T(8,128)} %bitcast.163) | data formatting | bytes 31457280
  123.9 10.5 fusion.53
  134.4 78.5 %fusion = f32[8,32768]{1,0:T(8,128)} fusion(f32[20,32768]{1,0:T(8,128)S(1)} %fusion.53), kind=kCustom, calls=%all-reduce-scatter | all-reduce-scatter fusion | flops 1048577 | bytes 3670528
  212.9 1.5 collective-permute-start
  214.4 1.3 slice.54
  215.7 2.6 collective-permute-start.1
  219.0 20.1 %collective-permute-done.1 = f32[1,32768]{1,0:T(1,128)S(1)} collective-permute-done((f32[1,32768]{1,0:T(1,128)S(1)}, f32[1,32768]{1,0:T(1,128)S(1)}, u32[]{:S(2)}, u32[]{:S(2)}) %collective-permute-start.1) | collective-permute-done | bytes 131104
  239.1 21.2 %concatenate.3 = f32[17,32768]{1,0:T(8,128)} concatenate(f32[1,32768]{1,0:T(1,128)S(1)} %collective-permute-done.1, f32[8,32768]{1,0:T(8,128)S(1)} %collective-permute-done, f32[8,32768]{1,0:T(8,128)} %fusion), dimensions={0} | concatenate | bytes 4456448
  260.3 1.7 constant_dynamic-slice_fusion.5
  262.4 2.2 fusion.29
  264.6 129.0 %all-reduce.11.cloned.1.call-done = f32[256,256]{0,1:T(8,128)} async-done(((f32[256,256]{0,1:T(8,128)}), f32[256,256]{0,1:T(8,128)}) %all-reduce.11.cloned.1.call-update) | async-done | bytes 262160 | tf_op jit(solution)/shard_map/psum | solution.py:65
  395.7 11.7 %cholesky.214 = f32[128,128]{1,0:T(8,128)S(1)} custom-call(f32[128,128]{1,0:T(8,128)S(1)} %cholesky.346), custom_call_target="Cholesky" | custom-call | tf_op jit(solution)/shard_map/jit(cholesky)/cholesky | solution.py:15
  407.5 9.8 custom-call.17
  417.8 11.7 %cholesky.231 = f32[128,128]{1,0:T(8,128)S(1)} custom-call(f32[128,128]{1,0:T(8,128)S(1)} %convolution_subtract_fusion.7), custom_call_target="Cholesky" | custom-call | tf_op jit(solution)/shard_map/jit(cholesky)/cholesky | solution.py:15
  431.8 15.1 %while.8 = (s32[]{:T(128)}, f32[256,256]{1,0:T(8,128)S(1)}, s32[2,2]{1,0:T(2,128)S(1)}, f32[2,128,128]{2,1,0:T(8,128)S(1)}, s32[]{:T(128)}) while((s32[]{:T(128)}, f32[256,256]{1,0:T(8,128)S(1)}, s32[2,2]{1,0:T(2,128)S(1)}, f32[2,128,128]{2,1,0:T(8,128)S(1)}, s32[]{:T(128)}) %tuple.83), condition=%wide.while_cond, body=%wide.while_body.sunk | while | flops 2 | bytes 131181 | solution.py:16
  443.4 1.4 bitcast_dynamic-update-slice_fusion.8
  445.5 1.4 bitcast_dynamic-update-slice_fusion.8
  446.9 19.7 %custom-call.18 = f32[2,128,128]{1,2,0:T(8,128)S(1)} custom-call(f32[2,128,128]{2,1,0:T(8,128)S(1)} %get-tuple-element.30), custom_call_target="InvertDiagBlocksLowerTriangular" | custom-call | tf_op jit(solution)/shard_map/jit(_solve_triangular)/triangular_solve | solution.py:16
  467.5 1.6 broadcast_multiply_fusion
  469.1 40.2 %all-gather.5.cloned.1.call-done = f32[5120,256]{1,0:T(8,128)} async-done(((f32[640,256]{1,0:T(8,128)}), f32[5120,256]{1,0:T(8,128)}) %all-gather.5.cloned.1.call-update) | async-done | bytes 5242896 | tf_op jit(solution)/shard_map/all_gather | solution.py:50
  509.3 12.1 %gather_fusion.1 = f32[120,128,256]{2,1,0:T(8,128)} fusion(f32[40,128,256]{2,1,0:T(8,128)} %bitcast.167, s32[1024]{0:T(1024)S(1)} %pad_clamp_fusion), kind=kCustom, calls=%fused_computation.1 | custom fusion | bytes 31457760 | tf_op jit(solution)/shard_map/gather | solution.py:52
  521.4 20.2 %convolution_bitcast_fusion = f32[120,128,256]{1,2,0:T(8,128)} fusion(f32[120,128,256]{2,1,0:T(8,128)} %gather_fusion.1, bf16[120,128,128]{2,1,0:T(8,128)(2,1)} %param.8), kind=kOutput, calls=%fused_computation.10 | convolution fusion | flops 6039797760 | bytes 35389440 | tf_op jit(solution)/shard_map/sij,sjk->sik/dot_general | solution.py:53
  541.6 15.7 %copy.42 = f32[15,8,128,256]{3,1,2,0:T(8,128)} copy(f32[15,8,128,256]{2,3,1,0:T(8,128)} %bitcast.165) | data formatting | bytes 31457280
  557.3 11.6 fusion.51
  568.9 78.6 %fusion.1 = f32[8,32768]{1,0:T(8,128)S(1)} fusion(f32[20,32768]{1,0:T(8,128)} %fusion.51), kind=kCustom, calls=%all-reduce-scatter.1 | all-reduce-scatter fusion | flops 1048577 | bytes 3670528
  647.4 2.3 collective-permute-start.2
  649.8 1.7 collective-permute-start.3
  651.5 1.9 fusion.82
  653.4 19.9 %collective-permute-done.3 = f32[1,32768]{1,0:T(1,128)S(1)} collective-permute-done((f32[1,32768]{1,0:T(1,128)S(1)}, f32[1,32768]{1,0:T(1,128)S(1)}, u32[]{:S(2)}, u32[]{:S(2)}) %collective-permute-start.3) | collective-permute-done | bytes 131104
  673.3 21.2 %concatenate.4 = f32[17,32768]{1,0:T(8,128)} concatenate(f32[1,32768]{1,0:T(1,128)S(1)} %collective-permute-done.3, f32[8,32768]{1,0:T(8,128)} %collective-permute-done.2, f32[8,32768]{1,0:T(8,128)S(1)} %fusion.1), dimensions={0} | concatenate | bytes 4456448
  694.5 1.7 constant_dynamic-slice_fusion.4
  696.6 2.1 fusion.30
  698.8 131.3 %all-reduce.15.cloned.1.call-done = (f32[256,256]{0,1:T(8,128)}, f32[256,256]{1,0:T(8,128)}) async-done(((f32[256,256]{0,1:T(8,128)}, f32[256,256]{1,0:T(8,128)}), (f32[256,256]{0,1:T(8,128)}, f32[256,256]{1,0:T(8,128)})) %all-reduce.15.cloned.1.call-update) | async-done | bytes 524304 | tf_op jit(solution)/shard_map/psum | solution.py:68
  832.2 11.7 %cholesky.248 = f32[128,128]{1,0:T(8,128)S(1)} custom-call(f32[128,128]{1,0:T(8,128)S(1)} %cholesky.349), custom_call_target="Cholesky" | custom-call | tf_op jit(solution)/shard_map/jit(cholesky)/cholesky | solution.py:15
  844.0 9.8 custom-call.19
  854.3 11.7 %cholesky.265 = f32[128,128]{1,0:T(8,128)S(1)} custom-call(f32[128,128]{1,0:T(8,128)S(1)} %convolution_subtract_fusion.6), custom_call_target="Cholesky" | custom-call | tf_op jit(solution)/shard_map/jit(cholesky)/cholesky | solution.py:15
  868.7 4.0 while.9
  869.3 1.4 bitcast_dynamic-update-slice_fusion.9
  871.3 1.4 bitcast_dynamic-update-slice_fusion.9
  872.7 19.8 %custom-call.20 = f32[2,128,128]{1,2,0:T(8,128)S(1)} custom-call(f32[2,128,128]{2,1,0:T(8,128)S(1)} %get-tuple-element.31), custom_call_target="InvertDiagBlocksLowerTriangular" | custom-call | tf_op jit(solution)/shard_map/jit(_solve_triangular)/triangular_solve | solution.py:16
  895.2 11.7 %cholesky.282 = f32[128,128]{1,0:T(8,128)S(1)} custom-call(f32[128,128]{1,0:T(8,128)S(1)} %cholesky.352), custom_call_target="Cholesky" | custom-call | tf_op jit(solution)/shard_map/jit(cholesky)/cholesky | solution.py:15
  907.0 9.8 custom-call.21
  917.3 11.9 %cholesky.299 = f32[128,128]{1,0:T(8,128)S(1)} custom-call(f32[128,128]{1,0:T(8,128)S(1)} %convolution_subtract_fusion.5), custom_call_target="Cholesky" | custom-call | tf_op jit(solution)/shard_map/jit(cholesky)/cholesky | solution.py:15
  931.8 4.0 while.10
  932.4 1.4 bitcast_dynamic-update-slice_fusion.10
  934.5 1.4 bitcast_dynamic-update-slice_fusion.10
  935.8 19.7 %custom-call.22 = f32[2,128,128]{1,2,0:T(8,128)S(1)} custom-call(f32[2,128,128]{2,1,0:T(8,128)S(1)} %get-tuple-element.32), custom_call_target="InvertDiagBlocksLowerTriangular" | custom-call | tf_op jit(solution)/shard_map/jit(_solve_triangular)/triangular_solve | solution.py:16
  957.2 1.9 fusion.83
  960.3 124.6 %all-reduce.13.cloned.1.call-done = f32[256,256]{0,1:T(8,128)} async-done(((f32[256,256]{0,1:T(8,128)}), f32[256,256]{0,1:T(8,128)}) %all-reduce.13.cloned.1.call-update) | async-done | bytes 262160 | tf_op jit(solution)/shard_map/psum | solution.py:83
  1087.0 11.7 %cholesky.316 = f32[128,128]{1,0:T(8,128)S(1)} custom-call(f32[128,128]{1,0:T(8,128)S(1)} %cholesky.355), custom_call_target="Cholesky" | custom-call | tf_op jit(solution)/shard_map/jit(cholesky)/cholesky | solution.py:15
  1098.8 9.8 custom-call.23
  1109.1 11.9 %cholesky.333 = f32[128,128]{1,0:T(8,128)S(1)} custom-call(f32[128,128]{1,0:T(8,128)S(1)} %convolution_subtract_fusion.4), custom_call_target="Cholesky" | custom-call | tf_op jit(solution)/shard_map/jit(cholesky)/cholesky | solution.py:15
  1123.8 4.1 while.11
  1124.4 1.4 bitcast_dynamic-update-slice_fusion.11
  1126.5 1.4 bitcast_dynamic-update-slice_fusion.11
  1127.9 19.7 %custom-call.24 = f32[2,128,128]{1,2,0:T(8,128)S(1)} custom-call(f32[2,128,128]{2,1,0:T(8,128)S(1)} %get-tuple-element.33), custom_call_target="InvertDiagBlocksLowerTriangular" | custom-call | tf_op jit(solution)/shard_map/jit(_solve_triangular)/triangular_solve | solution.py:16
  1148.5 1.6 convolution_multiply_fusion
  (111 shorter events, 27.2 us)
Async XLA Ops:
  7.2 29.4 %copy-start.3 = (s32[120]{0:T(128)S(1)}, s32[120]{0:T(128)}, u32[]{:S(2)}) copy-start(s32[120]{0:T(128)} %param.10) | copy-start | bytes 1444
  7.2 68.7 %all-gather.3.cloned.1.call-start = ((), (), s32[]{:S(2)}) async-start(), calls=%async_computation | async-start | bytes 5898240 | tf_op jit(solution)/shard_map/all_gather | solution.py:50
  36.5 357.1 %all-reduce.11.cloned.1.call-start = ((), (), s32[]{:S(2)}) async-start(), calls=%async_computation.1 | async-start | bytes 524288 | tf_op jit(solution)/shard_map/psum | solution.py:65
  108.2 15.7 %copy-start.2 = (s32[120]{0:T(128)S(1)}, s32[120]{0:T(128)}, u32[]{:S(2)}) copy-start(s32[120]{0:T(128)} %param.9) | copy-start | bytes 1444
  212.9 49.5 %copy-start = (f32[640,256]{1,0:T(8,128)S(1)}, f32[640,256]{1,0:T(8,128)}, u32[]{:S(2)}) copy-start(f32[640,256]{1,0:T(8,128)} %param.12) | copy-start | bytes 1966084
  212.9 26.2 %collective-permute-start = (f32[8,32768]{1,0:T(8,128)}, f32[8,32768]{1,0:T(8,128)S(1)}, u32[]{:S(2)}, u32[]{:S(2)}) collective-permute-start(f32[8,32768]{1,0:T(8,128)} %fusion), channel_id=1, source_target_pairs={{0,8},{8,16},{16,24},{1,9},{9,17},{17,25},{2,10},{10,18},{18,26},{... | collective-permute-start | bytes 3145736
  215.7 23.4 %collective-permute-start.1 = (f32[1,32768]{1,0:T(1,128)S(1)}, f32[1,32768]{1,0:T(1,128)S(1)}, u32[]{:S(2)}, u32[]{:S(2)}) collective-permute-start(f32[1,32768]{1,0:T(1,128)S(1)} %slice.54), channel_id=1, source_target_pairs={{0,16},{8,24},{1,17},{9,25},{2,18},{10,26},{3,19},{11,27},{4,20},{... | collective-permute-start | bytes 393224
  264.6 244.7 %all-gather.5.cloned.1.call-start = ((), (), s32[]{:S(2)}) async-start(), calls=%async_computation.2 | async-start | bytes 5898240 | tf_op jit(solution)/shard_map/all_gather | solution.py:50
  469.1 361.0 %all-reduce.15.cloned.1.call-start = ((), (), s32[]{:S(2)}) async-start(), calls=%async_computation.4 | async-start | bytes 1048576 | tf_op jit(solution)/shard_map/psum | solution.py:68
  647.4 25.9 %collective-permute-start.2 = (f32[8,32768]{1,0:T(8,128)S(1)}, f32[8,32768]{1,0:T(8,128)}, u32[]{:S(2)}, u32[]{:S(2)}) collective-permute-start(f32[8,32768]{1,0:T(8,128)S(1)} %fusion.1), channel_id=1, source_target_pairs={{0,8},{8,16},{16,24},{1,9},{9,17},{17,25},{2,10},{10,18},{18,26},{... | collective-permute-start | bytes 3145736
  649.8 23.5 %collective-permute-start.3 = (f32[1,32768]{1,0:T(1,128)S(1)}, f32[1,32768]{1,0:T(1,128)S(1)}, u32[]{:S(2)}, u32[]{:S(2)}) collective-permute-start(f32[1,32768]{1,0:T(1,128)S(1)} %slice.55), channel_id=1, source_target_pairs={{0,16},{8,24},{1,17},{9,25},{2,18},{10,26},{3,19},{11,27},{4,20},{... | collective-permute-start | bytes 393224
  698.7 386.2 %all-reduce.13.cloned.1.call-start = ((), (), s32[]{:S(2)}) async-start(), calls=%async_computation.3 | async-start | bytes 524288 | tf_op jit(solution)/shard_map/psum | solution.py:83
  830.1 64.1 %copy-start.1 = (f32[256,256]{1,0:T(8,128)S(1)}, f32[256,256]{1,0:T(8,128)}, u32[]{:S(2)}) copy-start(f32[256,256]{1,0:T(8,128)} %get-tuple-element.67) | copy-start | bytes 786436
Sparse Core Ops, SparseCore 0:
  36.7 39.1 all-gather.2
  264.7 128.9 all-reduce.10
  469.2 40.0 all-gather.4
  698.9 131.1 all-reduce.14
  959.2 125.6 all-reduce.12
where the time goes:
time: 1170 us; the launch traced here: 1160 us
  waiting for transfers between devices  504 us (43%)
  other arithmetic  227 us (19%)
  blocking collectives  177 us (15%)
  local copies, waits for them, and re-layouts  125 us (11%)
  matrix products  82.1 us (7%)
  between operations  22.1 us (2%)
    unnamed x3, blocking collectives  177 us
    another operation x27, other arithmetic, inverse_lower(): lower = jnp.linalg.cholesky(gram)  138 us
    psum x1, waiting for transfers between devices, body(): lax.psum((local_gram(raw_image), local_gram(pending)), ('col', 'row'))  131 us
    psum x1, waiting for transfers between devices, body(): inner_gram = lax.psum(local_gram(raw_image), ('col', 'row'))  129 us
    psum x1, waiting for transfers between devices, body(): final_gram = lax.psum(local_gram(pending), ('col', 'row'))  125 us
    unnamed x17, local copies, waits for them, and re-layouts  80.2 us
    all_gather x2, waiting for transfers between devices, body(): gathered = lax.all_gather(mapped_scaled, 'row', axis=0, tiled=True)  79.4 us
    another operation x9, other arithmetic, inverse_lower(): jax.scipy.linalg.solve_triangular(lower, jnp.eye(gram.shape[0], dtype=jnp...  79 us
  transfers between devices with their start and end apart: 9, of which 7 were waited for; matrix products, arithmetic and copies ran while one was open for 0% of the time, Pallas kernels for 0%

commit v1 on v0

--- a/solution.py
+++ b/solution.py
@@ -2,6 +2,7 @@
 import jax.numpy as jnp
 from jax import lax
 from jax.sharding import PartitionSpec as P
+from jax.lax import all_gather
 
 ITERS = 2
 highest = lax.Precision.HIGHEST
@@ -80,7 +81,11 @@
             )
         pending = apply_factor(image_block, inverse_lower(inner_gram))
         firsts.append(pending)
-    final_gram = lax.psum(local_gram(pending), ("col", "row"))
+
+    def show_cards(arr, group_axis):
+        return jnp.sum(all_gather(arr, group_axis), axis=0)
+
+    final_gram = show_cards(local_gram(pending), ("col", "row"))
     basis = apply_factor(pending, inverse_lower(final_gram))
     total_images = rows_local * n_row * n_col
     root = jnp.sqrt(jnp.float32(total_images))

time: 1170 us -> 1120 us (0.957)
  waiting for transfers between devices: 504 us -> 455 us
    psum x1 -> x0, waiting for transfers between devices: 125 us -> none  [body(): final_gram = lax.psum(local_gram(pending), ('col', 'row'))]
    all_gather x0 -> x1, waiting for transfers between devices: none -> 75 us  [show_cards(): return jnp.sum(all_gather(arr, group_axis), axis=0)]
where the time goes in v1:
time: 1120 us; the launch traced here: 1110 us
  waiting for transfers between devices  455 us (41%)
  other arithmetic  230 us (21%)
  blocking collectives  177 us (16%)
  local copies, waits for them, and re-layouts  124 us (11%)
  matrix products  82.2 us (7%)
  between operations  22.1 us (2%)
    unnamed x3, blocking collectives  177 us
    another operation x27, other arithmetic, inverse_lower(): lower = jnp.linalg.cholesky(gram)  138 us
    psum x1, waiting for transfers between devices, body(): lax.psum((local_gram(raw_image), local_gram(pending)), ('col', 'row'))  131 us
    psum x1, waiting for transfers between devices, body(): inner_gram = lax.psum(local_gram(raw_image), ('col', 'row'))  129 us
    unnamed x17, local copies, waits for them, and re-layouts  80.2 us
    all_gather x2, waiting for transfers between devices, body(): gathered = lax.all_gather(mapped_scaled, 'row', axis=0, tiled=True)  79.4 us
    another operation x9, other arithmetic, inverse_lower(): jax.scipy.linalg.solve_triangular(lower, jnp.eye(gram.shape[0], dtype=jnp...  79 us
    all_gather x1, waiting for transfers between devices, show_cards(): return jnp.sum(all_gather(arr, group_axis), axis=0)  75 us
  transfers between devices with their start and end apart: 9, of which 7 were waited for; matrix products, arithmetic and copies ran while one was open for 0% of the time, Pallas kernels for 0%

profile of v1, /device:TPU:0, one launch (start us, length us, event | category | flops | bytes accessed | tf_op | source)
XLA Modules:
  0.0 1109.5 jit_solution(18070264037895639692)
XLA Ops:
  7.9 3.2 convert_reduce_fusion
  11.9 20.4 %all-reduce.1 = f32[20,128]{1,0:T(8,128)S(1)} all-reduce(f32[20,128]{1,0:T(8,128)S(1)} %fusion.55), channel_id=3, replica_groups=mesh['col'=4,'row'=8] {'col'}, use_global_device_ids=true, to_apply=%region_1.0.clone | all-reduce | flops 2560 | bytes 20480
  32.4 1.4 fusion.81
  34.4 2.1 broadcast_multiply_fusion.1
  36.6 39.3 %all-gather.5.cloned.1.call-done = f32[5120,256]{1,0:T(8,128)} async-done(((f32[640,256]{1,0:T(8,128)}), f32[5120,256]{1,0:T(8,128)}) %all-gather.5.cloned.1.call-update) | async-done | bytes 5242896 | tf_op jit(solution)/shard_map/all_gather | solution.py:51
  75.9 12.1 %gather_fusion = f32[120,128,256]{2,1,0:T(8,128)} fusion(f32[40,128,256]{2,1,0:T(8,128)} %bitcast.167, s32[1024]{0:T(1024)S(1)} %pad_clamp_fusion), kind=kCustom, calls=%fused_computation | custom fusion | bytes 31457760 | tf_op jit(solution)/shard_map/gather | solution.py:53
  88.0 20.2 %convolution_bitcast_fusion.1 = f32[120,128,256]{1,2,0:T(8,128)} fusion(f32[120,128,256]{2,1,0:T(8,128)} %gather_fusion, bf16[120,128,128]{2,1,0:T(8,128)(2,1)} %param.8), kind=kOutput, calls=%fused_computation.11 | convolution fusion | flops 6039797760 | bytes 35389440 | tf_op jit(solution)/shard_map/sij,sjk->sik/dot_general | solution.py:54
  108.2 15.7 %copy.37 = f32[15,8,128,256]{3,1,2,0:T(8,128)} copy(f32[15,8,128,256]{2,3,1,0:T(8,128)} %bitcast.164) | data formatting | bytes 31457280
  123.9 10.5 fusion.53
  134.4 78.5 %fusion = f32[8,32768]{1,0:T(8,128)} fusion(f32[20,32768]{1,0:T(8,128)S(1)} %fusion.53), kind=kCustom, calls=%all-reduce-scatter | all-reduce-scatter fusion | flops 1048577 | bytes 3670528
  212.9 1.5 collective-permute-start
  215.7 2.6 collective-permute-start.1
  219.0 20.1 %collective-permute-done.1 = f32[1,32768]{1,0:T(1,128)S(1)} collective-permute-done((f32[1,32768]{1,0:T(1,128)S(1)}, f32[1,32768]{1,0:T(1,128)S(1)}, u32[]{:S(2)}, u32[]{:S(2)}) %collective-permute-start.1) | collective-permute-done | bytes 131104
  239.1 21.2 %concatenate.3 = f32[17,32768]{1,0:T(8,128)} concatenate(f32[1,32768]{1,0:T(1,128)S(1)} %collective-permute-done.1, f32[8,32768]{1,0:T(8,128)S(1)} %collective-permute-done, f32[8,32768]{1,0:T(8,128)} %fusion), dimensions={0} | concatenate | bytes 4456448
  260.3 1.7 constant_dynamic-slice_fusion.5
  262.4 2.2 fusion.29
  264.6 129.0 %all-reduce.10.cloned.1.call-done = f32[256,256]{0,1:T(8,128)} async-done(((f32[256,256]{0,1:T(8,128)}), f32[256,256]{0,1:T(8,128)}) %all-reduce.10.cloned.1.call-update) | async-done | bytes 262160 | tf_op jit(solution)/shard_map/psum | solution.py:66
  395.7 11.7 %cholesky.214 = f32[128,128]{1,0:T(8,128)S(1)} custom-call(f32[128,128]{1,0:T(8,128)S(1)} %cholesky.346), custom_call_target="Cholesky" | custom-call | tf_op jit(solution)/shard_map/jit(cholesky)/cholesky | solution.py:16
  407.5 9.8 custom-call.17
  417.8 11.7 %cholesky.231 = f32[128,128]{1,0:T(8,128)S(1)} custom-call(f32[128,128]{1,0:T(8,128)S(1)} %convolution_subtract_fusion.7), custom_call_target="Cholesky" | custom-call | tf_op jit(solution)/shard_map/jit(cholesky)/cholesky | solution.py:16
  431.8 15.1 %while.8 = (s32[]{:T(128)}, f32[256,256]{1,0:T(8,128)S(1)}, s32[2,2]{1,0:T(2,128)S(1)}, f32[2,128,128]{2,1,0:T(8,128)S(1)}, s32[]{:T(128)}) while((s32[]{:T(128)}, f32[256,256]{1,0:T(8,128)S(1)}, s32[2,2]{1,0:T(2,128)S(1)}, f32[2,128,128]{2,1,0:T(8,128)S(1)}, s32[]{:T(128)}) %tuple.83), condition=%wide.while_cond, body=%wide.while_body.sunk | while | flops 2 | bytes 131181 | solution.py:17
  443.4 1.4 bitcast_dynamic-update-slice_fusion.8
  445.5 1.4 bitcast_dynamic-update-slice_fusion.8
  446.9 19.7 %custom-call.18 = f32[2,128,128]{1,2,0:T(8,128)S(1)} custom-call(f32[2,128,128]{2,1,0:T(8,128)S(1)} %get-tuple-element.30), custom_call_target="InvertDiagBlocksLowerTriangular" | custom-call | tf_op jit(solution)/shard_map/jit(_solve_triangular)/triangular_solve | solution.py:17
  467.5 1.6 broadcast_multiply_fusion
  469.1 40.2 %all-gather.7.cloned.1.call-done = f32[5120,256]{1,0:T(8,128)} async-done(((f32[640,256]{1,0:T(8,128)}), f32[5120,256]{1,0:T(8,128)}) %all-gather.7.cloned.1.call-update) | async-done | bytes 5242896 | tf_op jit(solution)/shard_map/all_gather | solution.py:51
  509.3 12.1 %gather_fusion.1 = f32[120,128,256]{2,1,0:T(8,128)} fusion(f32[40,128,256]{2,1,0:T(8,128)} %bitcast.168, s32[1024]{0:T(1024)S(1)} %pad_clamp_fusion), kind=kCustom, calls=%fused_computation.1 | custom fusion | bytes 31457760 | tf_op jit(solution)/shard_map/gather | solution.py:53
  521.4 20.2 %convolution_bitcast_fusion = f32[120,128,256]{1,2,0:T(8,128)} fusion(f32[120,128,256]{2,1,0:T(8,128)} %gather_fusion.1, bf16[120,128,128]{2,1,0:T(8,128)(2,1)} %param.8), kind=kOutput, calls=%fused_computation.10 | convolution fusion | flops 6039797760 | bytes 35389440 | tf_op jit(solution)/shard_map/sij,sjk->sik/dot_general | solution.py:54
  541.6 15.7 %copy.38 = f32[15,8,128,256]{3,1,2,0:T(8,128)} copy(f32[15,8,128,256]{2,3,1,0:T(8,128)} %bitcast.166) | data formatting | bytes 31457280
  557.3 11.6 %fusion.51 = f32[20,32768]{1,0:T(8,128)} fusion(f32[120,32768]{1,0:T(8,128)} %bitcast.163, f32[120]{0:T(128)S(1)} %compare_convert_fusion, s32[120]{0:T(128)S(1)} %copy-done.2), kind=kOutput, calls=%fused_computation.109 | convolution fusion | flops 943723200 | bytes 18351040 | tf_op jit(solution)/shard_map/dot_general | solution.py:57
  568.9 78.6 %fusion.1 = f32[8,32768]{1,0:T(8,128)S(1)} fusion(f32[20,32768]{1,0:T(8,128)} %fusion.51), kind=kCustom, calls=%all-reduce-scatter.1 | all-reduce-scatter fusion | flops 1048577 | bytes 3670528
  647.4 2.3 collective-permute-start.2
  649.8 1.7 collective-permute-start.3
  651.5 1.9 fusion.82
  653.4 19.9 %collective-permute-done.3 = f32[1,32768]{1,0:T(1,128)S(1)} collective-permute-done((f32[1,32768]{1,0:T(1,128)S(1)}, f32[1,32768]{1,0:T(1,128)S(1)}, u32[]{:S(2)}, u32[]{:S(2)}) %collective-permute-start.3) | collective-permute-done | bytes 131104
  673.3 21.2 %concatenate.4 = f32[17,32768]{1,0:T(8,128)} concatenate(f32[1,32768]{1,0:T(1,128)S(1)} %collective-permute-done.3, f32[8,32768]{1,0:T(8,128)} %collective-permute-done.2, f32[8,32768]{1,0:T(8,128)S(1)} %fusion.1), dimensions={0} | concatenate | bytes 4456448
  694.5 1.7 constant_dynamic-slice_fusion.4
  696.6 2.1 fusion.30
  698.8 131.3 %all-reduce.12.cloned.1.call-done = (f32[256,256]{0,1:T(8,128)}, f32[256,256]{1,0:T(8,128)}) async-done(((f32[256,256]{0,1:T(8,128)}, f32[256,256]{1,0:T(8,128)}), (f32[256,256]{0,1:T(8,128)}, f32[256,256]{1,0:T(8,128)})) %all-reduce.12.cloned.1.call-update) | async-done | bytes 524304 | tf_op jit(solution)/shard_map/psum | solution.py:69
  832.2 11.7 %cholesky.248 = f32[128,128]{1,0:T(8,128)S(1)} custom-call(f32[128,128]{1,0:T(8,128)S(1)} %cholesky.349), custom_call_target="Cholesky" | custom-call | tf_op jit(solution)/shard_map/jit(cholesky)/cholesky | solution.py:16
  844.0 9.8 custom-call.19
  854.3 11.7 %cholesky.265 = f32[128,128]{1,0:T(8,128)S(1)} custom-call(f32[128,128]{1,0:T(8,128)S(1)} %convolution_subtract_fusion.6), custom_call_target="Cholesky" | custom-call | tf_op jit(solution)/shard_map/jit(cholesky)/cholesky | solution.py:16
  868.7 4.0 while.9
  869.3 1.4 bitcast_dynamic-update-slice_fusion.9
  871.3 1.4 bitcast_dynamic-update-slice_fusion.9
  872.7 19.8 %custom-call.20 = f32[2,128,128]{1,2,0:T(8,128)S(1)} custom-call(f32[2,128,128]{2,1,0:T(8,128)S(1)} %get-tuple-element.31), custom_call_target="InvertDiagBlocksLowerTriangular" | custom-call | tf_op jit(solution)/shard_map/jit(_solve_triangular)/triangular_solve | solution.py:17
  895.2 11.7 %cholesky.282 = f32[128,128]{1,0:T(8,128)S(1)} custom-call(f32[128,128]{1,0:T(8,128)S(1)} %cholesky.352), custom_call_target="Cholesky" | custom-call | tf_op jit(solution)/shard_map/jit(cholesky)/cholesky | solution.py:16
  907.0 9.8 custom-call.21
  917.3 11.9 %cholesky.299 = f32[128,128]{1,0:T(8,128)S(1)} custom-call(f32[128,128]{1,0:T(8,128)S(1)} %convolution_subtract_fusion.5), custom_call_target="Cholesky" | custom-call | tf_op jit(solution)/shard_map/jit(cholesky)/cholesky | solution.py:16
  931.8 4.0 while.10
  932.4 1.4 bitcast_dynamic-update-slice_fusion.10
  934.5 1.4 bitcast_dynamic-update-slice_fusion.10
  935.8 19.7 %custom-call.22 = f32[2,128,128]{1,2,0:T(8,128)S(1)} custom-call(f32[2,128,128]{2,1,0:T(8,128)S(1)} %get-tuple-element.32), custom_call_target="InvertDiagBlocksLowerTriangular" | custom-call | tf_op jit(solution)/shard_map/jit(_solve_triangular)/triangular_solve | solution.py:17
  957.2 1.9 fusion.83
  960.3 75.0 %all-gather.9.cloned.1.call-done = f32[8192,256]{1,0:T(8,128)} async-done(((f32[256,256]{1,0:T(8,128)}), f32[8192,256]{1,0:T(8,128)}) %all-gather.9.cloned.1.call-update) | async-done | bytes 8388624 | tf_op jit(solution)/shard_map/all_gather | solution.py:86
  1035.3 3.9 reduce_sum.19
  1039.4 11.7 %cholesky.316 = f32[128,128]{1,0:T(8,128)S(1)} custom-call(f32[128,128]{1,0:T(8,128)S(1)} %cholesky.355), custom_call_target="Cholesky" | custom-call | tf_op jit(solution)/shard_map/jit(cholesky)/cholesky | solution.py:16
  1051.2 9.8 custom-call.23
  1061.5 11.9 %cholesky.333 = f32[128,128]{1,0:T(8,128)S(1)} custom-call(f32[128,128]{1,0:T(8,128)S(1)} %convolution_subtract_fusion.4), custom_call_target="Cholesky" | custom-call | tf_op jit(solution)/shard_map/jit(cholesky)/cholesky | solution.py:16
  1076.2 4.1 while.11
  1076.9 1.4 bitcast_dynamic-update-slice_fusion.11
  1078.9 1.4 bitcast_dynamic-update-slice_fusion.11
  1080.4 19.7 %custom-call.24 = f32[2,128,128]{1,2,0:T(8,128)S(1)} custom-call(f32[2,128,128]{2,1,0:T(8,128)S(1)} %get-tuple-element.33), custom_call_target="InvertDiagBlocksLowerTriangular" | custom-call | tf_op jit(solution)/shard_map/jit(_solve_triangular)/triangular_solve | solution.py:17
  1101.0 1.6 convolution_multiply_fusion
  (112 shorter events, 26.6 us)
Async XLA Ops:
  7.2 29.4 %copy-start.3 = (s32[120]{0:T(128)S(1)}, s32[120]{0:T(128)}, u32[]{:S(2)}) copy-start(s32[120]{0:T(128)} %param.10) | copy-start | bytes 1444
  7.2 68.7 %all-gather.5.cloned.1.call-start = ((), (), s32[]{:S(2)}) async-start(), calls=%async_computation | async-start | bytes 5898240 | tf_op jit(solution)/shard_map/all_gather | solution.py:51
  36.5 357.1 %all-reduce.10.cloned.1.call-start = ((), (), s32[]{:S(2)}) async-start(), calls=%async_computation.1 | async-start | bytes 524288 | tf_op jit(solution)/shard_map/psum | solution.py:66
  108.2 15.7 %copy-start.2 = (s32[120]{0:T(128)S(1)}, s32[120]{0:T(128)}, u32[]{:S(2)}) copy-start(s32[120]{0:T(128)} %param.9) | copy-start | bytes 1444
  212.9 49.5 %copy-start = (f32[640,256]{1,0:T(8,128)S(1)}, f32[640,256]{1,0:T(8,128)}, u32[]{:S(2)}) copy-start(f32[640,256]{1,0:T(8,128)} %param.12) | copy-start | bytes 1966084
  212.9 26.2 %collective-permute-start = (f32[8,32768]{1,0:T(8,128)}, f32[8,32768]{1,0:T(8,128)S(1)}, u32[]{:S(2)}, u32[]{:S(2)}) collective-permute-start(f32[8,32768]{1,0:T(8,128)} %fusion), channel_id=1, source_target_pairs={{0,8},{8,16},{16,24},{1,9},{9,17},{17,25},{2,10},{10,18},{18,26},{... | collective-permute-start | bytes 3145736
  215.7 23.4 %collective-permute-start.1 = (f32[1,32768]{1,0:T(1,128)S(1)}, f32[1,32768]{1,0:T(1,128)S(1)}, u32[]{:S(2)}, u32[]{:S(2)}) collective-permute-start(f32[1,32768]{1,0:T(1,128)S(1)} %slice.54), channel_id=1, source_target_pairs={{0,16},{8,24},{1,17},{9,25},{2,18},{10,26},{3,19},{11,27},{4,20},{... | collective-permute-start | bytes 393224
  264.6 244.7 %all-gather.7.cloned.1.call-start = ((), (), s32[]{:S(2)}) async-start(), calls=%async_computation.2 | async-start | bytes 5898240 | tf_op jit(solution)/shard_map/all_gather | solution.py:51
  469.1 361.0 %all-reduce.12.cloned.1.call-start = ((), (), s32[]{:S(2)}) async-start(), calls=%async_computation.4 | async-start | bytes 1048576 | tf_op jit(solution)/shard_map/psum | solution.py:69
  647.4 25.9 %collective-permute-start.2 = (f32[8,32768]{1,0:T(8,128)S(1)}, f32[8,32768]{1,0:T(8,128)}, u32[]{:S(2)}, u32[]{:S(2)}) collective-permute-start(f32[8,32768]{1,0:T(8,128)S(1)} %fusion.1), channel_id=1, source_target_pairs={{0,8},{8,16},{16,24},{1,9},{9,17},{17,25},{2,10},{10,18},{18,26},{... | collective-permute-start | bytes 3145736
  649.8 23.5 %collective-permute-start.3 = (f32[1,32768]{1,0:T(1,128)S(1)}, f32[1,32768]{1,0:T(1,128)S(1)}, u32[]{:S(2)}, u32[]{:S(2)}) collective-permute-start(f32[1,32768]{1,0:T(1,128)S(1)} %slice.55), channel_id=1, source_target_pairs={{0,16},{8,24},{1,17},{9,25},{2,18},{10,26},{3,19},{11,27},{4,20},{... | collective-permute-start | bytes 393224
  698.7 336.6 %all-gather.9.cloned.1.call-start = ((), (), s32[]{:S(2)}) async-start(), calls=%async_computation.3 | async-start | bytes 8650752 | tf_op jit(solution)/shard_map/all_gather | solution.py:86
  830.1 64.1 %copy-start.1 = (f32[256,256]{1,0:T(8,128)S(1)}, f32[256,256]{1,0:T(8,128)}, u32[]{:S(2)}) copy-start(f32[256,256]{1,0:T(8,128)} %get-tuple-element.67) | copy-start | bytes 786436
Sparse Core Ops, SparseCore 0:
  36.7 39.1 all-gather.4
  264.7 128.9 all-reduce.9
  469.2 40.0 all-gather.6
  698.9 131.1 all-reduce.11
  959.3 76.0 all-gather.8
